TPU v7x, 32 devices: a whole 2x2x4 slice. The times are simulated.
32 devices in a mesh: groups: 2 (over x), samples: 16 (over z, y, core).
Axes of the slice: x: 2, y: 2, z: 4, core: 2. Of those that a mesh axis runs over, the one named last changes fastest.
Arguments:
- terms: float32 [1048576, 64], P(('groups', 'samples')), parts along dimension 0
- coefficients: float32 [64, 256], replicated, may hold values from -1.5 to 1.5
- counts: int32 [512], P('groups'), parts along dimension 0, may hold values from 1 to 4095, as said below
- labels: int32 [1048576], P(('groups', 'samples')), parts along dimension 0, may hold values from 0 to 255, as said below
- f_start: float32 [512], P('groups'), parts along dimension 0, may hold values from -8 to 8
Outputs:
- free: float32 [512], P('groups'), parts along dimension 0
- intersection: float32 [512, 256], P(('groups', 'samples')), parts along dimension 0
- anchor_mix: float32 [512, 256], P(('groups', 'samples')), parts along dimension 0
- term_means: float32 [512, 64], P(('groups', 'samples')), parts along dimension 0
There are 2 independent parts, one for each index of `groups`. A program takes and returns all parts, laid end to end along the dimension named above; an argument that names none is the same for every part. Nothing has to cross between parts.
Inputs may be any that keep to these rules, and one draw needn't show every extreme that they name: counts sum to 524288. `labels`: exactly counts[k] snapshots carry the label k.
All inputs are finite; a program needn't handle non-finite values.
Results may differ from a plain program's by a relative error of at most 0.0003.
Values sent between devices are 32-bit elements; how exact they have to be, the bound alone decides.
A program may use at most 128 MiB of HBM per device.

v0:
```python
import jax
import jax.numpy as jnp
from jax import lax
from jax.sharding import PartitionSpec as P

ITERS = 4


def energies(block, coefficients):
    return jnp.dot(
        block, coefficients, precision=lax.Precision.HIGHEST, preferred_element_type=jnp.float32
    )


def denominator(energy, free_now, log_counts):
    shifted = log_counts[None, :] + free_now[None, :] - energy
    top = jnp.max(shifted, axis=1, keepdims=True)
    return top[:, 0] + jnp.log(jnp.sum(jnp.exp(shifted - top), axis=1))


def local(terms, coefficients, counts, labels, f_start):
    rows = terms.shape[0]
    states = coefficients.shape[1]
    block_rows = min(4096, rows)
    blocks = terms.reshape(rows // block_rows, block_rows, terms.shape[1])
    label_blocks = labels.reshape(rows // block_rows, block_rows)
    log_counts = jnp.log(counts.astype(jnp.float32))
    scaled_counts = counts.astype(jnp.float32)
    free_now = f_start
    for step in range(ITERS):

        def accumulate(carry, block):
            peak, total = carry
            energy = energies(block, coefficients)
            denom = denominator(energy, free_now, log_counts)
            logw = -energy - denom[:, None]
            new_peak = jnp.maximum(peak, jnp.max(logw, axis=0))
            total = total * jnp.exp(peak - new_peak) + jnp.sum(
                jnp.exp(logw - new_peak[None, :]), axis=0
            )
            return ((new_peak, total), None)

        init = (jnp.full((states,), -1e30, jnp.float32), jnp.zeros((states,), jnp.float32))
        (peak, total), _ = lax.scan(accumulate, init, blocks)
        highest = lax.pmax(peak, "samples")
        total = lax.psum(total * jnp.exp(peak - highest), "samples")
        peak = highest
        updated = -(peak + jnp.log(total))
        free_now = updated - updated[0]
    state_ids = jnp.arange(states, dtype=jnp.int32)

    def diagnose(carry, pair):
        over, anchor, term_sum, weight_sum = carry
        block, label_block = pair
        energy = energies(block, coefficients)
        denom = denominator(energy, free_now, log_counts)
        weight = jnp.exp(free_now[None, :] - energy - denom[:, None])
        over = over + jnp.dot(
            weight.T,
            weight * scaled_counts[None, :],
            precision=lax.Precision.HIGHEST,
            preferred_element_type=jnp.float32,
        )
        onehot = (label_block[:, None] == state_ids[None, :]).astype(jnp.float32)
        anchor = anchor + jnp.dot(
            onehot.T, weight, precision=lax.Precision.HIGHEST, preferred_element_type=jnp.float32
        )
        term_sum = term_sum + jnp.dot(
            weight.T, block, precision=lax.Precision.HIGHEST, preferred_element_type=jnp.float32
        )
        weight_sum = weight_sum + jnp.sum(weight, axis=0)
        return ((over, anchor, term_sum, weight_sum), None)

    init = (
        jnp.zeros((states, states), jnp.float32),
        jnp.zeros((states, states), jnp.float32),
        jnp.zeros((states, terms.shape[1]), jnp.float32),
        jnp.zeros((states,), jnp.float32),
    )
    (over, anchor, term_sum, weight_sum), _ = lax.scan(diagnose, init, (blocks, label_blocks))
    over, anchor, term_sum, weight_sum = lax.psum((over, anchor, term_sum, weight_sum), "samples")
    owned = states // lax.axis_size("samples")
    first_row = lax.axis_index("samples") * owned
    over = lax.dynamic_slice_in_dim(over, first_row, owned, 0)
    anchor = lax.dynamic_slice_in_dim(anchor, first_row, owned, 0)
    term_sum = lax.dynamic_slice_in_dim(term_sum, first_row, owned, 0)
    weight_sum = lax.dynamic_slice_in_dim(weight_sum, first_row, owned, 0)
    return (free_now, over, anchor, term_sum / weight_sum[:, None])


def solution(mesh):
    return jax.shard_map(
        local,
        mesh=mesh,
        in_specs=(
            P(("groups", "samples"), None),
            P(),
            P("groups"),
            P(("groups", "samples")),
            P("groups"),
        ),
        out_specs=(
            P("groups"),
            P(("groups", "samples"), None),
            P(("groups", "samples"), None),
            P(("groups", "samples"), None),
        ),
        check_vma=False,
    )
```

profile of v0, /device:TPU:0, one launch (start us, length us, event | category | flops | bytes accessed | tf_op | source)
XLA Modules:
  0.0 897.7 jit_solution(15325472563780318898)
XLA Ops:
  7.4 12.3 %copy.9 = f32[32768,64]{1,0:T(8,128)} copy(f32[32768,64]{0,1:T(8,128)} %param.15) | data formatting | bytes 16777216 | tf_op args[0]
  19.7 84.8 %while.79 = (s32[]{:T(128)}, f32[256]{0:T(256)S(1)}, f32[256]{0:T(256)S(1)}, f32[8,4096,64]{2,1,0:T(8,128)}, f32[64,256]{1,0:T(8,128)S(1)}, /*index=5*/f32[1,256]{1,0:T(1,128)S(1)}, s32[]{:T(128)}, s32[]{:T(128)}) while((s32[]{:T(128)}, f32[256]{0:T(256)S(1)}, f32[256]{0:T(256)S(1)}, f32[8,4096,64]{2,1,0:T(8,128)}, ...), condition=%wide.region_5.6_spmd.clone, body=%wide.region_0.5_spmd.clone.sunk | while | flops 817886464 | bytes 35864184 | solution.py:44
  19.7 5.2 subtract_reduce_fusion.10
  30.3 5.2 subtract_reduce_fusion.10
  51.5 5.2 subtract_reduce_fusion.10
  62.1 5.2 subtract_reduce_fusion.10
  83.3 5.2 subtract_reduce_fusion.10
  93.9 5.2 subtract_reduce_fusion.10
  104.5 35.0 %pmax.28 = f32[256]{0:T(256)S(1)} all-reduce(f32[256]{0:T(256)S(1)} %get-tuple-element.470), channel_id=1, replica_groups=mesh['groups'=2,'samples'=16] {'samples'}, use_global_device_ids=true, to_apply=%region_6.7 | all-reduce | flops 256 | bytes 2048 | tf_op jit(solution)/shard_map/pmax | solution.py:45
  139.4 29.5 %psum.56 = f32[256]{0:T(256)S(1)} all-reduce(f32[256]{0:T(256)S(1)} %exponential_multiply_fusion.3), channel_id=1, replica_groups=mesh['groups'=2,'samples'=16] {'samples'}, use_global_device_ids=true, to_apply=%region_7.8 | all-reduce | flops 256 | bytes 2048 | tf_op jit(solution)/shard_map/psum | solution.py:46
  170.0 84.8 %while.80 = (s32[]{:T(128)}, f32[256]{0:T(256)S(1)}, f32[256]{0:T(256)S(1)}, f32[8,4096,64]{2,1,0:T(8,128)}, f32[64,256]{1,0:T(8,128)S(1)}, /*index=5*/f32[1,256]{1,0:T(1,128)S(1)}, s32[]{:T(128)}, s32[]{:T(128)}) while((s32[]{:T(128)}, f32[256]{0:T(256)S(1)}, f32[256]{0:T(256)S(1)}, f32[8,4096,64]{2,1,0:T(8,128)}, ...), condition=%wide.region_13.14_spmd.clone, body=%wide.region_8.13_spmd.clone.sunk | while | flops 817886464 | bytes 35864184 | solution.py:44
  191.2 5.2 subtract_reduce_fusion.11
  233.6 5.2 subtract_reduce_fusion.11
  254.8 29.5 %pmax.29 = f32[256]{0:T(256)S(1)} all-reduce(f32[256]{0:T(256)S(1)} %get-tuple-element.472), channel_id=1, replica_groups=mesh['groups'=2,'samples'=16] {'samples'}, use_global_device_ids=true, to_apply=%region_14.15 | all-reduce | flops 256 | bytes 2048 | tf_op jit(solution)/shard_map/pmax | solution.py:45
  284.3 29.7 %psum.57 = f32[256]{0:T(256)S(1)} all-reduce(f32[256]{0:T(256)S(1)} %exponential_multiply_fusion.2), channel_id=1, replica_groups=mesh['groups'=2,'samples'=16] {'samples'}, use_global_device_ids=true, to_apply=%region_15.16 | all-reduce | flops 256 | bytes 2048 | tf_op jit(solution)/shard_map/psum | solution.py:46
  315.1 84.8 %while.81 = (s32[]{:T(128)}, f32[256]{0:T(256)S(1)}, f32[256]{0:T(256)S(1)}, f32[8,4096,64]{2,1,0:T(8,128)}, f32[64,256]{1,0:T(8,128)S(1)}, /*index=5*/f32[1,256]{1,0:T(1,128)S(1)}, s32[]{:T(128)}, s32[]{:T(128)}) while((s32[]{:T(128)}, f32[256]{0:T(256)S(1)}, f32[256]{0:T(256)S(1)}, f32[8,4096,64]{2,1,0:T(8,128)}, ...), condition=%wide.region_21.22_spmd.clone, body=%wide.region_16.21_spmd.clone.sunk | while | flops 817886464 | bytes 35864184 | solution.py:44
  399.9 29.5 %pmax.30 = f32[256]{0:T(256)S(1)} all-reduce(f32[256]{0:T(256)S(1)} %get-tuple-element.474), channel_id=1, replica_groups=mesh['groups'=2,'samples'=16] {'samples'}, use_global_device_ids=true, to_apply=%region_22.23 | all-reduce | flops 256 | bytes 2048 | tf_op jit(solution)/shard_map/pmax | solution.py:45
  429.4 29.5 %psum.58 = f32[256]{0:T(256)S(1)} all-reduce(f32[256]{0:T(256)S(1)} %exponential_multiply_fusion.1), channel_id=1, replica_groups=mesh['groups'=2,'samples'=16] {'samples'}, use_global_device_ids=true, to_apply=%region_23.24 | all-reduce | flops 256 | bytes 2048 | tf_op jit(solution)/shard_map/psum | solution.py:46
  460.1 84.9 %while.82 = (s32[]{:T(128)}, f32[256]{0:T(256)S(1)}, f32[256]{0:T(256)S(1)}, f32[8,4096,64]{2,1,0:T(8,128)}, f32[64,256]{1,0:T(8,128)S(1)}, /*index=5*/f32[1,256]{1,0:T(1,128)S(1)}, s32[]{:T(128)}, s32[]{:T(128)}) while((s32[]{:T(128)}, f32[256]{0:T(256)S(1)}, f32[256]{0:T(256)S(1)}, f32[8,4096,64]{2,1,0:T(8,128)}, ...), condition=%wide.region_29.30_spmd.clone, body=%wide.region_24.29_spmd.clone.sunk | while | flops 817886464 | bytes 35864184 | solution.py:44
  460.1 5.2 subtract_reduce_fusion.13
  470.7 5.2 subtract_reduce_fusion.13
  481.3 5.2 subtract_reduce_fusion.13
  491.9 5.2 subtract_reduce_fusion.13
  502.5 5.2 subtract_reduce_fusion.13
  513.1 5.2 subtract_reduce_fusion.13
  523.7 5.2 subtract_reduce_fusion.13
  534.3 5.2 subtract_reduce_fusion.13
  544.9 29.5 %pmax.31 = f32[256]{0:T(256)S(1)} all-reduce(f32[256]{0:T(256)S(1)} %get-tuple-element.476), channel_id=1, replica_groups=mesh['groups'=2,'samples'=16] {'samples'}, use_global_device_ids=true, to_apply=%region_30.31 | all-reduce | flops 256 | bytes 2048 | tf_op jit(solution)/shard_map/pmax | solution.py:45
  574.4 29.5 %psum.59 = f32[256]{0:T(256)S(1)} all-reduce(f32[256]{0:T(256)S(1)} %exponential_multiply_fusion), channel_id=1, replica_groups=mesh['groups'=2,'samples'=16] {'samples'}, use_global_device_ids=true, to_apply=%region_31.32 | all-reduce | flops 256 | bytes 2048 | tf_op jit(solution)/shard_map/psum | solution.py:46
  605.2 192.2 %while.83 = (s32[]{:T(128)}, f32[256,256]{1,0:T(8,128)S(1)}, f32[256,256]{1,0:T(8,128)S(1)}, f32[256,64]{0,1:T(8,128)S(1)}, f32[256]{0:T(256)S(1)}, /*index=5*/f...) while((s32[]{:T(128)}, f32[256,256]{1,0:T(8,128)S(1)}, ...), condition=%wide.region_36.37_spmd.clone, body=%wide.region_32.36_spmd.clone.sunk | while | flops 8073277952 | bytes 64385216 | solution.py:80
  605.4 5.3 subtract_reduce_fusion.14
  613.5 7.2 fusion.106
  629.4 5.3 subtract_reduce_fusion.14
  637.5 7.2 fusion.106
  653.4 5.3 subtract_reduce_fusion.14
  661.5 7.2 fusion.106
  677.4 5.3 subtract_reduce_fusion.14
  685.5 7.2 fusion.106
  701.4 5.3 subtract_reduce_fusion.14
  709.5 7.2 fusion.106
  725.4 5.3 subtract_reduce_fusion.14
  733.5 7.2 fusion.106
  749.4 5.3 subtract_reduce_fusion.14
  757.5 7.2 fusion.106
  773.4 5.3 subtract_reduce_fusion.14
  781.5 7.2 fusion.106
  798.2 29.7 %psum.63 = f32[256]{0:T(256)S(1)} all-reduce(f32[256]{0:T(256)S(1)} %get-tuple-element.481), channel_id=1, replica_groups=mesh['groups'=2,'samples'=16] {'samples'}, use_global_device_ids=true, to_apply=%region_40.41 | all-reduce | flops 256 | bytes 2048 | tf_op jit(solution)/shard_map/psum | solution.py:81
  828.0 59.8 %all-reduce.3.cloned.1.call-done = (f32[256,256]{1,0:T(8,128)}, f32[256,256]{1,0:T(8,128)}, f32[256,64]{1,0:T(8,128)}) async-done(((f32[256,256]{1,0:T(8,128)}, f32[256,256]{1,0:T(8,128)}, f32[256,64]{1,0:T(8,128)}), (f32[256,256]{1,0:T(8,128)}, f32[256,256]{1,0:T(8,128)}, f32[256,64]{1,0:T(8,128)})) %all-reduce.3.cloned.1.call-update) | async-done | bytes 589840 | tf_op jit(solution)/shard_map/psum | solution.py:81
  (443 shorter events, 353.1 us)
Async XLA Ops:
  7.2 880.6 %all-reduce.3.cloned.1.call-start = ((), (), s32[]{:S(2)}) async-start(), calls=%async_computation | async-start | bytes 1310720 | tf_op jit(solution)/shard_map/psum | solution.py:81
  7.3 12.3 %copy-start.11 = (s32[256]{0:T(256)S(1)}, s32[256]{0:T(256)}, u32[]{:S(2)}) copy-start(s32[256]{0:T(256)} %param.17) | copy-start | bytes 3076
  7.3 12.3 %copy-start.12 = (f32[256]{0:T(256)S(1)}, f32[256]{0:T(256)}, u32[]{:S(2)}) copy-start(f32[256]{0:T(256)} %param.19) | copy-start | bytes 3076
  7.3 12.3 %copy-start.6 = (f32[64,256]{1,0:T(8,128)S(1)}, f32[64,256]{1,0:T(8,128)}, u32[]{:S(2)}) copy-start(f32[64,256]{1,0:T(8,128)} %param.16) | copy-start | bytes 196612
  24.8 1.9 copy-start.2
  35.4 1.9 copy-start.2
  46.0 1.9 copy-start.2
  56.6 1.9 copy-start.2
  67.2 1.9 copy-start.2
  77.8 1.9 copy-start.2
  88.4 1.9 copy-start.2
  99.0 1.9 copy-start.2
  175.2 1.9 copy-start.3
  185.8 1.9 copy-start.3
  196.4 1.9 copy-start.3
  207.0 1.9 copy-start.3
  217.6 1.9 copy-start.3
  228.2 1.9 copy-start.3
  238.8 1.9 copy-start.3
  249.4 1.9 copy-start.3
  320.3 1.9 copy-start.4
  330.9 1.9 copy-start.4
  341.5 1.9 copy-start.4
  352.1 1.9 copy-start.4
  362.7 1.9 copy-start.4
  373.3 1.9 copy-start.4
  383.9 1.9 copy-start.4
  394.5 1.9 copy-start.4
  460.1 145.0 %copy-start.9 = (s32[32768]{0:T(1024)S(1)}, s32[32768]{0:T(1024)}, u32[]{:S(2)}) copy-start(s32[32768]{0:T(1024)} %param.18) | copy-start | bytes 393220
  465.3 1.9 copy-start.5
  475.9 1.9 copy-start.5
  486.5 1.9 copy-start.5
  497.1 1.9 copy-start.5
  507.7 1.9 copy-start.5
  518.3 1.9 copy-start.5
  528.9 1.9 copy-start.5
  539.5 1.9 copy-start.5
  613.5 7.3 copy-start.1
  637.5 7.3 copy-start.1
  658.7 1.9 copy-start
  661.5 7.3 copy-start.1
  682.7 1.9 copy-start
  685.5 7.3 copy-start.1
  709.5 7.3 copy-start.1
  733.5 7.3 copy-start.1
  757.5 7.3 copy-start.1
  781.5 7.3 copy-start.1
  797.4 93.1 %copy-start.10 = (f32[256]{0:T(256)}, f32[256]{0:T(256)S(1)}, u32[]{:S(2)}) copy-start(f32[256]{0:T(256)S(1)} %get-tuple-element.1079) | copy-start | bytes 3076
  (8 other events, 13.2 us)
Sparse Core Ops, SparseCore 0:
  798.4 89.3 all-reduce.2
where the time goes:
time: 908 us; the launch traced here: 898 us
  matrix products  335 us (37%)
  blocking collectives  271 us (30%)
  other arithmetic  176 us (19%)
  waiting for transfers between devices  59.8 us (7%)
  local copies, waits for them, and re-layouts  38.3 us (4%)
  between operations  14.7 us (2%)
    dot_general x40, matrix products, energies(): jnp.dot(block, coefficients, precision=lax.Precision.HIGHEST, preferred_e...  208 us
    pmax x4, blocking collectives, local(): highest = lax.pmax(peak, 'samples')  123 us
    psum x4, blocking collectives, local(): total = lax.psum(total * jnp.exp(peak - highest), 'samples')  118 us
    reduce_sum x32, other arithmetic, accumulate(): jnp.sum(jnp.exp(logw - new_peak[None, :]), axis=0)  87 us
    psum x1, waiting for transfers between devices, local(): lax.psum((over, anchor, term_sum, weight_sum), 'samples')  59.8 us
    dot_general x8, matrix products, diagnose(): jnp.dot(weight.T, block, precision=lax.Precision.HIGHEST, preferred_eleme...  57.9 us
    reduce_sum x40, other arithmetic, denominator(): return top[:, 0] + jnp.log(jnp.sum(jnp.exp(shifted - top), axis=1))  54.4 us
    dot_general x8, matrix products, diagnose(): jnp.dot(weight.T, weight * scaled_counts[None, :], precision=lax.Precisio...  39 us
  transfers between devices with their start and end apart: 1, of which 1 were waited for; matrix products, arithmetic and copies ran while one was open for 0% of the time, Pallas kernels for 0%

commit v1 on v0

--- a/solution.py
+++ b/solution.py
@@ -43,7 +43,9 @@
         init = (jnp.full((states,), -1e30, jnp.float32), jnp.zeros((states,), jnp.float32))
         (peak, total), _ = lax.scan(accumulate, init, blocks)
         highest = lax.pmax(peak, "samples")
-        total = lax.psum(total * jnp.exp(peak - highest), "samples")
+        body = total * jnp.exp(peak - highest)
+        r_now = lax.all_gather(body, axis_name="samples")
+        total = jnp.sum(r_now, 0)
         peak = highest
         updated = -(peak + jnp.log(total))
         free_now = updated - updated[0]

time: 908 us -> 866 us (0.954)
  blocking collectives: 271 us -> 230 us
    psum x4 -> x0, blocking collectives: 118 us -> none  [local(): total = lax.psum(total * jnp.exp(peak - highest), 'samples')]
    all_gather x0 -> x4, blocking collectives: none -> 68.8 us  [local(): r_now = lax.all_gather(body, axis_name='samples')]
where the time goes in v1:
time: 866 us; the launch traced here: 856 us
  matrix products  335 us (39%)
  blocking collectives  230 us (27%)
  other arithmetic  176 us (20%)
  waiting for transfers between devices  59.3 us (7%)
  local copies, waits for them, and re-layouts  38.3 us (4%)
  between operations  14.7 us (2%)
    dot_general x40, matrix products, energies(): jnp.dot(block, coefficients, precision=lax.Precision.HIGHEST, preferred_e...  208 us
    pmax x4, blocking collectives, local(): highest = lax.pmax(peak, 'samples')  129 us
    reduce_sum x32, other arithmetic, accumulate(): jnp.sum(jnp.exp(logw - new_peak[None, :]), axis=0)  87 us
    all_gather x4, blocking collectives, local(): r_now = lax.all_gather(body, axis_name='samples')  68.8 us
    psum x1, waiting for transfers between devices, local(): lax.psum((over, anchor, term_sum, weight_sum), 'samples')  59.3 us
    dot_general x8, matrix products, diagnose(): jnp.dot(weight.T, block, precision=lax.Precision.HIGHEST, preferred_eleme...  58 us
    reduce_sum x40, other arithmetic, denominator(): return top[:, 0] + jnp.log(jnp.sum(jnp.exp(shifted - top), axis=1))  54.4 us
    dot_general x8, matrix products, diagnose(): jnp.dot(weight.T, weight * scaled_counts[None, :], precision=lax.Precisio...  39 us
  transfers between devices with their start and end apart: 1, of which 1 were waited for; matrix products, arithmetic and copies ran while one was open for 0% of the time, Pallas kernels for 0%

profile of v1, /device:TPU:0, one launch (start us, length us, event | category | flops | bytes accessed | tf_op | source)
XLA Modules:
  0.0 855.8 jit_solution(17649505619400609874)
XLA Ops:
  7.4 12.3 %copy.11 = f32[32768,64]{1,0:T(8,128)} copy(f32[32768,64]{0,1:T(8,128)} %param.15) | data formatting | bytes 16777216 | tf_op args[0]
  19.7 84.8 %while.79 = (s32[]{:T(128)}, f32[256]{0:T(256)S(1)}, f32[256]{0:T(256)S(1)}, f32[8,4096,64]{2,1,0:T(8,128)}, f32[64,256]{1,0:T(8,128)S(1)}, /*index=5*/f32[1,256]{1,0:T(1,128)S(1)}, s32[]{:T(128)}, s32[]{:T(128)}) while((s32[]{:T(128)}, f32[256]{0:T(256)S(1)}, f32[256]{0:T(256)S(1)}, f32[8,4096,64]{2,1,0:T(8,128)}, ...), condition=%wide.region_5.6_spmd.clone, body=%wide.region_0.5_spmd.clone.sunk | while | flops 817886464 | bytes 35864184 | solution.py:44
  19.7 5.2 subtract_reduce_fusion.10
  30.3 5.2 subtract_reduce_fusion.10
  51.5 5.2 subtract_reduce_fusion.10
  62.1 5.2 subtract_reduce_fusion.10
  93.9 5.2 subtract_reduce_fusion.10
  104.5 35.0 %pmax.28 = f32[256]{0:T(256)S(1)} all-reduce(f32[256]{0:T(256)S(1)} %get-tuple-element.470), channel_id=1, replica_groups=mesh['groups'=2,'samples'=16] {'samples'}, use_global_device_ids=true, to_apply=%region_6.7 | all-reduce | flops 256 | bytes 2048 | tf_op jit(solution)/shard_map/pmax | solution.py:45
  139.4 17.2 %all-gather.4 = f32[16,1,256]{2,1,0:T(1,128)S(1)} all-gather(f32[1,1,256]{2,1,0:T(1,128)S(1)} %bitcast.105), channel_id=2, replica_groups=mesh['groups'=2,'samples'=16] {'samples'}, dimensions={0}, use_global_device_ids=true | all-gather | bytes 17408 | tf_op jit(solution)/shard_map/all_gather | solution.py:47
  157.7 84.8 %while.80 = (s32[]{:T(128)}, f32[256]{0:T(256)S(1)}, f32[256]{0:T(256)S(1)}, f32[8,4096,64]{2,1,0:T(8,128)}, f32[64,256]{1,0:T(8,128)S(1)}, /*index=5*/f32[1,256]{1,0:T(1,128)S(1)}, s32[]{:T(128)}, s32[]{:T(128)}) while((s32[]{:T(128)}, f32[256]{0:T(256)S(1)}, f32[256]{0:T(256)S(1)}, f32[8,4096,64]{2,1,0:T(8,128)}, ...), condition=%wide.region_13.14_spmd.clone, body=%wide.region_8.13_spmd.clone.sunk | while | flops 817886464 | bytes 35864184 | solution.py:44
  189.5 5.2 subtract_reduce_fusion.11
  210.7 5.2 subtract_reduce_fusion.11
  242.5 31.4 %pmax.29 = f32[256]{0:T(256)S(1)} all-reduce(f32[256]{0:T(256)S(1)} %get-tuple-element.472), channel_id=1, replica_groups=mesh['groups'=2,'samples'=16] {'samples'}, use_global_device_ids=true, to_apply=%region_14.15 | all-reduce | flops 256 | bytes 2048 | tf_op jit(solution)/shard_map/pmax | solution.py:45
  273.9 17.3 %all-gather.5 = f32[16,1,256]{2,1,0:T(1,128)S(1)} all-gather(f32[1,1,256]{2,1,0:T(1,128)S(1)} %bitcast.106), channel_id=3, replica_groups=mesh['groups'=2,'samples'=16] {'samples'}, dimensions={0}, use_global_device_ids=true | all-gather | bytes 17408 | tf_op jit(solution)/shard_map/all_gather | solution.py:47
  292.5 84.8 %while.81 = (s32[]{:T(128)}, f32[256]{0:T(256)S(1)}, f32[256]{0:T(256)S(1)}, f32[8,4096,64]{2,1,0:T(8,128)}, f32[64,256]{1,0:T(8,128)S(1)}, /*index=5*/f32[1,256]{1,0:T(1,128)S(1)}, s32[]{:T(128)}, s32[]{:T(128)}) while((s32[]{:T(128)}, f32[256]{0:T(256)S(1)}, f32[256]{0:T(256)S(1)}, f32[8,4096,64]{2,1,0:T(8,128)}, ...), condition=%wide.region_21.22_spmd.clone, body=%wide.region_16.21_spmd.clone.sunk | while | flops 817886464 | bytes 35864184 | solution.py:44
  292.5 5.2 subtract_reduce_fusion.12
  377.2 31.4 %pmax.30 = f32[256]{0:T(256)S(1)} all-reduce(f32[256]{0:T(256)S(1)} %get-tuple-element.474), channel_id=1, replica_groups=mesh['groups'=2,'samples'=16] {'samples'}, use_global_device_ids=true, to_apply=%region_22.23 | all-reduce | flops 256 | bytes 2048 | tf_op jit(solution)/shard_map/pmax | solution.py:45
  408.7 17.2 %all-gather.6 = f32[16,1,256]{2,1,0:T(1,128)S(1)} all-gather(f32[1,1,256]{2,1,0:T(1,128)S(1)} %bitcast.107), channel_id=4, replica_groups=mesh['groups'=2,'samples'=16] {'samples'}, dimensions={0}, use_global_device_ids=true | all-gather | bytes 17408 | tf_op jit(solution)/shard_map/all_gather | solution.py:47
  427.1 84.8 %while.82 = (s32[]{:T(128)}, f32[256]{0:T(256)S(1)}, f32[256]{0:T(256)S(1)}, f32[8,4096,64]{2,1,0:T(8,128)}, f32[64,256]{1,0:T(8,128)S(1)}, /*index=5*/f32[1,256]{1,0:T(1,128)S(1)}, s32[]{:T(128)}, s32[]{:T(128)}) while((s32[]{:T(128)}, f32[256]{0:T(256)S(1)}, f32[256]{0:T(256)S(1)}, f32[8,4096,64]{2,1,0:T(8,128)}, ...), condition=%wide.region_29.30_spmd.clone, body=%wide.region_24.29_spmd.clone.sunk | while | flops 817886464 | bytes 35864184 | solution.py:44
  427.1 5.2 subtract_reduce_fusion.13
  437.7 5.2 subtract_reduce_fusion.13
  448.3 5.2 subtract_reduce_fusion.13
  458.9 5.2 subtract_reduce_fusion.13
  469.5 5.2 subtract_reduce_fusion.13
  480.1 5.2 subtract_reduce_fusion.13
  490.7 5.2 subtract_reduce_fusion.13
  501.3 5.2 subtract_reduce_fusion.13
  511.9 31.4 %pmax.31 = f32[256]{0:T(256)S(1)} all-reduce(f32[256]{0:T(256)S(1)} %get-tuple-element.476), channel_id=1, replica_groups=mesh['groups'=2,'samples'=16] {'samples'}, use_global_device_ids=true, to_apply=%region_30.31 | all-reduce | flops 256 | bytes 2048 | tf_op jit(solution)/shard_map/pmax | solution.py:45
  543.3 17.2 %all-gather.7 = f32[16,1,256]{2,1,0:T(1,128)S(1)} all-gather(f32[1,1,256]{2,1,0:T(1,128)S(1)} %bitcast.108), channel_id=5, replica_groups=mesh['groups'=2,'samples'=16] {'samples'}, dimensions={0}, use_global_device_ids=true | all-gather | bytes 17408 | tf_op jit(solution)/shard_map/all_gather | solution.py:47
  561.8 192.2 %while.83 = (s32[]{:T(128)}, f32[256,256]{1,0:T(8,128)S(1)}, f32[256,256]{1,0:T(8,128)S(1)}, f32[256,64]{0,1:T(8,128)S(1)}, f32[256]{0:T(256)S(1)}, /*index=5*/f...) while((s32[]{:T(128)}, f32[256,256]{1,0:T(8,128)S(1)}, ...), condition=%wide.region_36.37_spmd.clone, body=%wide.region_32.36_spmd.clone.sunk | while | flops 8073277952 | bytes 64385216 | solution.py:82
  562.0 5.3 subtract_reduce_fusion.14
  570.1 7.2 fusion.106
  586.0 5.3 subtract_reduce_fusion.14
  594.1 7.2 fusion.106
  610.0 5.3 subtract_reduce_fusion.14
  618.1 7.2 fusion.106
  634.0 5.3 subtract_reduce_fusion.14
  642.1 7.2 fusion.106
  658.0 5.3 subtract_reduce_fusion.14
  666.1 7.2 fusion.106
  682.0 5.3 subtract_reduce_fusion.14
  690.1 7.2 fusion.106
  706.0 5.3 subtract_reduce_fusion.14
  714.1 7.2 fusion.106
  730.0 5.3 subtract_reduce_fusion.14
  738.1 7.2 fusion.106
  754.9 31.5 %psum.31 = f32[256]{0:T(256)S(1)} all-reduce(f32[256]{0:T(256)S(1)} %get-tuple-element.481), channel_id=1, replica_groups=mesh['groups'=2,'samples'=16] {'samples'}, use_global_device_ids=true, to_apply=%region_40.41 | all-reduce | flops 256 | bytes 2048 | tf_op jit(solution)/shard_map/psum | solution.py:83
  786.5 59.3 %all-reduce.3.cloned.1.call-done = (f32[256,256]{1,0:T(8,128)}, f32[256,256]{1,0:T(8,128)}, f32[256,64]{1,0:T(8,128)}) async-done(((f32[256,256]{1,0:T(8,128)}, f32[256,256]{1,0:T(8,128)}, f32[256,64]{1,0:T(8,128)}), (f32[256,256]{1,0:T(8,128)}, f32[256,256]{1,0:T(8,128)}, f32[256,64]{1,0:T(8,128)})) %all-reduce.3.cloned.1.call-update) | async-done | bytes 589840 | tf_op jit(solution)/shard_map/psum | solution.py:83
  (447 shorter events, 353.3 us)
Async XLA Ops:
  7.2 838.7 %all-reduce.3.cloned.1.call-start = ((), (), s32[]{:S(2)}) async-start(), calls=%async_computation | async-start | bytes 1310720 | tf_op jit(solution)/shard_map/psum | solution.py:83
  7.3 12.3 %copy-start.11 = (s32[256]{0:T(256)S(1)}, s32[256]{0:T(256)}, u32[]{:S(2)}) copy-start(s32[256]{0:T(256)} %param.17) | copy-start | bytes 3076
  7.3 12.3 %copy-start.12 = (f32[256]{0:T(256)S(1)}, f32[256]{0:T(256)}, u32[]{:S(2)}) copy-start(f32[256]{0:T(256)} %param.19) | copy-start | bytes 3076
  7.3 12.3 %copy-start.6 = (f32[64,256]{1,0:T(8,128)S(1)}, f32[64,256]{1,0:T(8,128)}, u32[]{:S(2)}) copy-start(f32[64,256]{1,0:T(8,128)} %param.16) | copy-start | bytes 196612
  24.8 1.9 copy-start.2
  35.4 1.9 copy-start.2
  46.0 1.9 copy-start.2
  56.6 1.9 copy-start.2
  67.2 1.9 copy-start.2
  77.8 1.9 copy-start.2
  88.4 1.9 copy-start.2
  99.0 1.9 copy-start.2
  162.9 1.9 copy-start.3
  173.5 1.9 copy-start.3
  184.1 1.9 copy-start.3
  194.7 1.9 copy-start.3
  205.3 1.9 copy-start.3
  215.9 1.9 copy-start.3
  226.5 1.9 copy-start.3
  237.1 1.9 copy-start.3
  297.7 1.9 copy-start.4
  308.3 1.9 copy-start.4
  318.9 1.9 copy-start.4
  329.5 1.9 copy-start.4
  340.0 1.9 copy-start.4
  350.6 1.9 copy-start.4
  361.2 1.9 copy-start.4
  371.8 1.9 copy-start.4
  427.0 134.7 %copy-start.9 = (s32[32768]{0:T(1024)S(1)}, s32[32768]{0:T(1024)}, u32[]{:S(2)}) copy-start(s32[32768]{0:T(1024)} %param.18) | copy-start | bytes 393220
  432.3 1.9 copy-start.5
  442.9 1.9 copy-start.5
  453.5 1.9 copy-start.5
  464.1 1.9 copy-start.5
  474.7 1.9 copy-start.5
  485.3 1.9 copy-start.5
  495.9 1.9 copy-start.5
  506.5 1.9 copy-start.5
  570.1 7.3 copy-start.1
  591.3 1.9 copy-start
  594.1 7.3 copy-start.1
  615.3 1.9 copy-start
  618.1 7.3 copy-start.1
  642.1 7.3 copy-start.1
  666.1 7.3 copy-start.1
  690.1 7.3 copy-start.1
  714.1 7.3 copy-start.1
  738.1 7.3 copy-start.1
  754.0 94.5 %copy-start.10 = (f32[256]{0:T(256)}, f32[256]{0:T(256)S(1)}, u32[]{:S(2)}) copy-start(f32[256]{0:T(256)S(1)} %get-tuple-element.1079) | copy-start | bytes 3076
  (8 other events, 13.2 us)
Sparse Core Ops, SparseCore 0:
  755.0 90.7 all-reduce.2
